TPU v7x, 32 devices: a whole 2x2x4 slice. The times are simulated.
32 devices in a mesh: fsdp: 8 (over y, x, core), sp: 4 (over z).
Axes of the slice: x: 2, y: 2, z: 4, core: 2. Of those that a mesh axis runs over, the one named last changes fastest.
Arguments:
- tokens_in: bfloat16 [8, 1024, 1536], P('fsdp', 'sp')
- w_qkv: bfloat16 [1536, 3, 16, 128], P('fsdp', None, 'sp')
- grad_attn: bfloat16 [8, 1024, 16, 128], P('fsdp', None, 'sp'), may hold values from -6 to 6
- kv_tiles: int32 [16, 8, 4], P('sp'), may hold values from 0 to 7, as said below
- tile_live: int32 [16, 8, 4], P('sp'), may hold values from 0 to 1, as said below
Outputs:
- attention_out: bfloat16 [8, 1024, 16, 128], P('fsdp', None, 'sp')
- grad_tokens: bfloat16 [8, 1024, 1536], P('fsdp', 'sp')
Inputs may be any that keep to these rules, and one draw needn't show every extreme that they name: `kv_tiles`: in every row the first slot names the query tile itself; the live tiles of one row are distinct. `tile_live`: the first slot of every row is live.
All inputs are finite; a program needn't handle non-finite values.
Results may differ from a plain program's by a relative error of at most 0.014.
The roundings to bfloat16 on the way count: a program that leaves them out, or rounds other values in their place, can miss the bound.
Values may be sent and summed in bfloat16 or wider, within the bound.
No kernel may reach another device: no remote copies, remote signals or barrier semaphores. Data moves between devices by JAX's collectives and lax.ppermute only.
A program may use at most 128 MiB of HBM per device.

v0:
```python
import functools

import jax
import jax.numpy as jnp
from jax import lax
from jax.experimental import pallas as pl
from jax.experimental.pallas import tpu as pltpu
from jax.sharding import PartitionSpec as P


HEAD = 128
TILE = 128
NN = (((1,), (0,)), ((), ()))
NT = (((1,), (1,)), ((), ()))


PAUSE = 4400
LOG2E = 1.4426950408889634


def dot(a, b, dims):
    return lax.dot_general(a, b, dims, preferred_element_type=jnp.float32)


def groups(slots):
    return [range(s, min(s + 2, slots)) for s in range(0, slots, 2)]


def weave(*streams):
    streams = [stream for stream in streams if stream is not None]
    while streams:
        streams = [stream for stream in streams if next(stream, None) is not None]


def project_kernel(*refs, keys, parts):
    shards = len(keys)
    mine = lax.axis_index("fsdp")
    shard_refs, part_refs = refs[:shards], refs[shards : shards + parts]
    w_ref, qkv_ref = refs[shards + parts :]
    rows, width = shard_refs[0].shape
    block = 4 * HEAD

    def fill(column):
        for place, shard in enumerate(shard_refs):
            at = pl.ds(pl.multiple_of((mine ^ keys[place]) * rows, rows), rows)
            w_ref[at, column : column + block] = shard[:, column : column + block]
            yield True

    def multiply(column):
        tokens = jnp.concatenate([part[...] for part in part_refs], axis=0)
        columns = slice(column, column + block)
        qkv_ref[:, columns] = dot(tokens, w_ref[:, columns], NN).astype(jnp.bfloat16)
        yield True

    weave(fill(0))
    for column in range(0, width, block):
        weave(fill(column + block) if column + block < width else None, multiply(column))


def project(keys, shards, parts):
    _, width = shards[0].shape
    depth = parts[0].shape[1]
    length = sum(part.shape[0] for part in parts)
    anywhere = pl.BlockSpec(memory_space=pl.ANY)
    return pl.pallas_call(
        functools.partial(project_kernel, keys=tuple(keys), parts=len(parts)),
        out_shape=(
            jax.ShapeDtypeStruct((depth, width), jnp.bfloat16),
            jax.ShapeDtypeStruct((length, width), jnp.bfloat16),
        ),
        in_specs=[pl.BlockSpec(memory_space=pltpu.VMEM)] * (len(shards) + len(parts)),
        out_specs=(pl.BlockSpec(memory_space=pltpu.VMEM),) * 2,
        name="project",
        cost_estimate=pl.CostEstimate(
            flops=2 * length * depth * width,
            bytes_accessed=4 * depth * width + 4 * length * width,
            transcendentals=0,
        ),
        compiler_params=pltpu.CompilerParams(vmem_limit_bytes=max(4 << 20, (2 << 20) + 2 * length * depth)),
    )(*shards, *parts)


def product_kernel(dqkv_ref, w_ref, *out_refs, start):
    def multiply(start, out_refs):
        rows = sum(out_ref.shape[0] for out_ref in out_refs)
        whole = dot(dqkv_ref[start : start + rows, :], w_ref[...], NT)
        at = 0
        for out_ref in out_refs:
            out_ref[...] = whole[at : at + out_ref.shape[0]]
            at += out_ref.shape[0]

    for number in range(0, len(out_refs) - 1, 2):
        multiply(start, out_refs[number : number + 2])
        start += 2 * out_refs[number].shape[0]
    multiply(0, out_refs[-1:])


def products(dqkv, w, start, sizes):
    depth, width = w.shape
    return pl.pallas_call(
        functools.partial(product_kernel, start=start),
        out_shape=tuple(jax.ShapeDtypeStruct((size, depth), jnp.float32) for size in sizes),
        name="products",
        cost_estimate=pl.CostEstimate(
            flops=2 * sum(sizes) * depth * width,
            bytes_accessed=2 * depth * width + 6 * sum(sizes) * depth,
            transcendentals=0,
        ),
        compiler_params=pltpu.CompilerParams(vmem_limit_bytes=4 << 20),
    )(dqkv, w)


def finish_kernel(own_ref, low_ref, high_ref, out_ref):
    half = low_ref.shape[0]
    out_ref[:half, :] = (own_ref[:half, :] + low_ref[...].astype(jnp.float32)).astype(jnp.bfloat16)
    out_ref[half:, :] = (own_ref[half:, :] + high_ref[...].astype(jnp.float32)).astype(jnp.bfloat16)


def finish(own, low, high):
    return pl.pallas_call(
        finish_kernel,
        out_shape=jax.ShapeDtypeStruct(own.shape, jnp.bfloat16),
        name="finish",
        compiler_params=pltpu.CompilerParams(vmem_limit_bytes=2 << 20),
    )(own, low, high)


def attention_kernel(
    packed_ref, early_ref, late_ref, last_ref, w_ref, dout_ref,
    out_ref, dqkv_ref, first_ref, second_ref, place_ref, qkv_ref, kt_ref, vt_ref, *refs,
    heads, all_slots, chunk,
):
    dkv_refs, score_refs, grad_refs, prob_refs, peak_refs = (
        refs[group * heads : (group + 1) * heads] for group in range(5)
    )
    sem = refs[5 * heads]
    length = qkv_ref.shape[0]
    width = heads * HEAD
    tile_count = length // TILE
    scale = HEAD ** (-0.5)
    early = early_ref.shape[0]
    copy = pltpu.make_async_copy(early_ref, qkv_ref.at[pl.ds(0, early)], sem)
    copy.start()
    per_chunk = chunk // TILE
    sp_count = length // chunk
    device = lax.axis_index("sp")
    spot = jnp.where(device % 2 == 0, device // 2, sp_count - 1 - device // 2)
    for number in range(sp_count):
        step = lax.rem(spot - ring_spot(number, sp_count) + sp_count, sp_count)
        for tile in range(per_chunk):
            place_ref[number * per_chunk + tile] = step * per_chunk + tile
    most = packed_ref[heads * tile_count * all_slots]

    def project_late():
        for column in range(0, 3 * width, 2 * HEAD):
            columns = slice(column, column + 2 * HEAD)
            tokens = jnp.concatenate([late_ref[...], last_ref[...]], axis=0)
            qkv_ref[early:, columns] = dot(tokens, w_ref[:, columns], NN).astype(jnp.bfloat16)
            yield True

    def turn_rows(start, stop):
        for head in range(heads):
            at = head * HEAD
            for row in range(start, stop, TILE):
                rows = slice(row, row + TILE)
                kt_ref[head, :, rows] = qkv_ref[rows, width + at : width + at + HEAD].T
                vt_ref[head, :, rows] = qkv_ref[rows, 2 * width + at : 2 * width + at + HEAD].T
                yield True

    def clear():
        for head in range(heads):
            for row in range(0, length, TILE):
                dkv_refs[head][row : row + TILE, :] = jnp.zeros((TILE, 2 * HEAD), jnp.float32)
                yield True

    weave(clear())
    copy.wait()
    weave(project_late(), turn_rows(0, early))
    weave(turn_rows(early, length))

    def tile_rows(tile):
        return pl.ds(pl.multiple_of(tile * TILE, TILE), TILE)

    def spots_of(head, tile, slots):
        base = (head * tile_count + tile) * all_slots
        return base, [tile_rows(place_ref[jnp.maximum(packed_ref[base + s], 0)]) for s in range(slots)]

    def operands(head, tile):
        at = head * HEAD
        query = qkv_ref[tile_rows(place_ref[tile]), at : at + HEAD]
        return query, dout_ref[tile_rows(tile), at : at + HEAD]

    def enter(slots, head, tile):
        at = head * HEAD
        base, spots = spots_of(head, tile, slots)
        query, dout = operands(head, tile)
        peak = None
        empty = jnp.zeros((TILE, HEAD), jnp.bfloat16)
        both = jnp.concatenate([jnp.concatenate([query, empty], axis=1), jnp.concatenate([empty, dout], axis=1)], axis=0)
        for group in groups(slots):
            lhs = [
                jnp.concatenate(
                    [
                        qkv_ref[spots[s], width + at : width + at + HEAD],
                        qkv_ref[spots[s], 2 * width + at : 2 * width + at + HEAD],
                    ],
                    axis=1,
                )
                for s in group
            ]
            parts = dot(jnp.concatenate(lhs, axis=0), both, NT)
            yield True
            for number, s in enumerate(group):
                part = parts[number * TILE : (number + 1) * TILE]
                score = part[:, :TILE]
                if s > 0:
                    score = jnp.where(packed_ref[base + s] >= 0, score, -1e30)
                score_refs[head][s * TILE : (s + 1) * TILE, :] = score
                grad_refs[head][s * TILE : (s + 1) * TILE, :] = part[:, TILE:]
                peak = score if peak is None else jnp.maximum(peak, score)
                yield True
        peak_refs[head][...] = jnp.broadcast_to(jnp.max(peak, axis=0, keepdims=True), (8, TILE))

    def middle(slots, head, tile):
        peak = peak_refs[head][:1, :]
        total = jnp.zeros((1, TILE), jnp.float32)
        delta = jnp.zeros((1, TILE), jnp.float32)
        for s in range(slots):
            part = slice(s * TILE, (s + 1) * TILE)
            grown = jnp.exp2((score_refs[head][part, :] - peak) * (scale * LOG2E))
            score_refs[head][part, :] = grown
            total += jnp.sum(grown, axis=0, keepdims=True)
            delta += jnp.sum(grown * grad_refs[head][part, :], axis=0, keepdims=True)
            yield True
        inverse = 1.0 / total
        delta = delta * inverse
        for s in range(slots):
            part = slice(s * TILE, (s + 1) * TILE)
            prob = score_refs[head][part, :] * inverse
            prob_refs[head][part, TILE:] = prob.astype(jnp.bfloat16)
            prob_refs[head][part, :TILE] = (prob * (grad_refs[head][part, :] - delta) * scale).astype(jnp.bfloat16)
            yield True

    def leave(slots, head, tile):
        at = head * HEAD
        rows = tile_rows(tile)
        held = tile_rows(place_ref[tile])
        _, spots = spots_of(head, tile, slots)
        query, dout = operands(head, tile)
        empty = jnp.zeros((TILE, HEAD), jnp.bfloat16)
        both = jnp.concatenate([jnp.concatenate([query, empty], axis=1), jnp.concatenate([empty, dout], axis=1)], axis=0)
        value_t = jnp.concatenate([vt_ref[head, :, spot] for spot in spots], axis=1)
        out_ref[rows, at : at + HEAD] = dot(value_t, prob_refs[head][: slots * TILE, TILE:], NN).T.astype(jnp.bfloat16)
        yield True
        key_t = jnp.concatenate([kt_ref[head, :, spot] for spot in spots], axis=1)
        dqkv_ref[held, at : at + HEAD] = dot(key_t, prob_refs[head][: slots * TILE, :TILE], NN).T.astype(jnp.bfloat16)
        yield True
        for group in groups(slots):
            parts = dot(prob_refs[head][group[0] * TILE : (group[-1] + 1) * TILE, :], both, NN)
            yield True
            for number, s in enumerate(group):
                dkv_refs[head][spots[s], :] += parts[number * TILE : (number + 1) * TILE]
                yield True

    def before(head, tile, back):
        order = head - back
        return (order % heads, tile + order // heads)

    def turn(slots, tile, first):
        for head in range(heads):
            weave(
                enter(slots, head, tile),
                middle(slots, *before(head, tile, 1)) if not first or head >= 1 else None,
                leave(slots, *before(head, tile, 2)) if not first or head >= 2 else None,
            )

    def run(slots):
        turn(slots, 0, True)

        def step(tile, carry):
            turn(slots, tile, False)
            return carry

        lax.fori_loop(1, tile_count, step, 0)
        last = tile_count - 1
        weave(middle(slots, heads - 1, last), leave(slots, *before(heads, last, 2)))
        weave(leave(slots, heads - 1, last))

    few = all_slots - 1
    if few > 0:
        pl.when(most <= few)(lambda: run(few))
        pl.when(most > few)(lambda: run(all_slots))
    else:
        run(all_slots)
    for head in range(heads):
        at = head * HEAD
        dqkv_ref[:, width + at : width + at + HEAD] = dkv_refs[head][:, :HEAD].astype(jnp.bfloat16)
        dqkv_ref[:, 2 * width + at : 2 * width + at + HEAD] = dkv_refs[head][:, HEAD:].astype(jnp.bfloat16)
    half = chunk // 2
    whole = dot(dqkv_ref[chunk : 2 * chunk, :], w_ref[...], NT).astype(jnp.bfloat16)
    first_ref[...] = whole[:half]
    second_ref[...] = whole[half:]


def attention(early, late, last, w, dout, codes, shape, chunk):
    length = dout.shape[0]
    heads, tile_count, slots = shape
    width = heads * HEAD
    depth = w.shape[0]
    smem = pl.BlockSpec(memory_space=pltpu.SMEM)
    vmem = pl.BlockSpec(memory_space=pltpu.VMEM)
    anywhere = pl.BlockSpec(memory_space=pl.ANY)
    return pl.pallas_call(
        functools.partial(attention_kernel, heads=heads, all_slots=slots, chunk=chunk),
        out_shape=(
            jax.ShapeDtypeStruct((length, width), jnp.bfloat16),
            jax.ShapeDtypeStruct((length, 3 * width), jnp.bfloat16),
            jax.ShapeDtypeStruct((chunk // 2, depth), jnp.bfloat16),
            jax.ShapeDtypeStruct((chunk // 2, depth), jnp.bfloat16),
        ),
        in_specs=[smem, anywhere, vmem, vmem, vmem, vmem],
        out_specs=(vmem, vmem, vmem, vmem),
        scratch_shapes=[
            pltpu.SMEM((tile_count,), jnp.int32),
            pltpu.VMEM((length, 3 * width), jnp.bfloat16),
            pltpu.VMEM((heads, HEAD, length), jnp.bfloat16),
            pltpu.VMEM((heads, HEAD, length), jnp.bfloat16),
        ]
        + [pltpu.VMEM((length, 2 * HEAD), jnp.float32)] * heads
        + [pltpu.VMEM((slots * TILE, TILE), jnp.float32)] * (2 * heads)
        + [pltpu.VMEM((slots * TILE, 2 * TILE), jnp.bfloat16)] * heads
        + [pltpu.VMEM((8, TILE), jnp.float32)] * heads
        + [pltpu.SemaphoreType.DMA],
        name="attention",
        cost_estimate=pl.CostEstimate(
            flops=12 * heads * tile_count * slots * TILE * TILE * HEAD,
            bytes_accessed=16 * length * width,
            transcendentals=heads * tile_count * slots * TILE * TILE,
        ),
        compiler_params=pltpu.CompilerParams(vmem_limit_bytes=18 << 20),
    )(codes, early, late, last, w, dout)


def pack_kernel(code_ref, dout_ref, packed_ref, *, slots):
    rows = code_ref.shape[0] // slots
    most = 1
    for base in range(0, rows * slots, slots):
        packed = [code_ref[base]] + [-1] * (slots - 1)
        count = 1
        for s in range(1, slots):
            code = code_ref[base + s]
            target = jnp.where(code >= 0, count, 0)
            for j in range(1, s + 1):
                packed[j] = jnp.where(target == j, code, packed[j])
            count = count + jnp.where(code >= 0, 1, 0)
        for s in range(slots):
            packed_ref[base + s] = packed[s]
        most = jnp.maximum(most, count)
    packed_ref[rows * slots] = most


def pack(codes, slots, dout):
    smem = pl.BlockSpec(memory_space=pltpu.SMEM)
    return pl.pallas_call(
        functools.partial(pack_kernel, slots=slots),
        out_shape=jax.ShapeDtypeStruct((codes.shape[0] + 1,), jnp.int32),
        in_specs=[smem, pl.BlockSpec(memory_space=pl.ANY)],
        out_specs=smem,
        name="pack",
        compiler_params=pltpu.CompilerParams(vmem_limit_bytes=1 << 20),
    )(codes, dout)


def stagger_kernel(out_ref):
    turns = (lax.axis_index("fsdp") % 2) * PAUSE
    out_ref[0] = lax.fori_loop(0, turns, lambda _, x: (x * 5 + 3) & 1023, turns)


def stagger():
    return pl.pallas_call(
        stagger_kernel,
        out_shape=jax.ShapeDtypeStruct((1,), jnp.int32),
        out_specs=pl.BlockSpec(memory_space=pltpu.SMEM),
        name="stagger",
        compiler_params=pltpu.CompilerParams(has_side_effects=True),
    )()


def ring_spot(device, count):
    return device // 2 if device % 2 == 0 else count - 1 - device // 2


def weight_bits(count):
    return [1 << b for b in range(1, count.bit_length() - 1)]


def gather_weights(w, axis, count):
    def swap(value, bit):
        return lax.ppermute(value, axis, [(i, i ^ bit) for i in range(count)])

    held = {0: w, 1: swap(w, 1)}
    bits = weight_bits(count)
    if len(bits) == 2:
        low, high = bits
        for k in range(2):
            held[low | k] = swap(held[k], low)
            held[high | k] = swap(held[k], high)
        held[low | high] = swap(held[high], low)
        held[low | high | 1] = swap(held[low | 1], high)
    else:
        for bit in bits:
            held.update({k | bit: swap(v, bit) for k, v in list(held.items())})
    return held


def make_shards(fsdp_count, sp_count):
    order = sorted(range(sp_count), key=lambda device: ring_spot(device, sp_count))
    ring = [(order[i], order[(i + 1) % sp_count]) for i in range(sp_count)]

    def layer(tokens_in, w_qkv, grad_attn, kv_tiles, tile_live):
        tokens = tokens_in[0]
        chunk, _ = tokens.shape
        half = chunk // 2
        heads, tile_count, _ = kv_tiles.shape
        length = tile_count * TILE
        width = heads * HEAD
        codes = jnp.where(tile_live > 0, kv_tiles, -1).reshape(-1)
        dout = grad_attn[0].reshape(length, width)
        codes = pack(codes, kv_tiles.shape[2], dout)
        held = gather_weights(w_qkv.reshape(w_qkv.shape[0], -1), "fsdp", fsdp_count)
        halves = [tokens[:half], tokens[half:]]
        parts = [tokens]
        for _ in range(1, sp_count):
            for side in range(2):
                halves[side] = lax.ppermute(halves[side], "sp", ring)
                parts.append(halves[side])
        stagger()
        w, early = project(list(held), list(held.values()), parts[:-2])
        out, dqkv, low, high = attention(
            early, parts[-2], parts[-1], w, dout, codes, kv_tiles.shape, chunk
        )
        sums = products(dqkv, w, 2 * chunk, [half] * (2 * sp_count - 4) + [chunk])
        for step in range(1, sp_count):
            if step > 1:
                low = (sums[2 * step - 4] + low.astype(jnp.float32)).astype(jnp.bfloat16)
            low = lax.ppermute(low, "sp", ring)
            if step > 1:
                high = (sums[2 * step - 3] + high.astype(jnp.float32)).astype(jnp.bfloat16)
            high = lax.ppermute(high, "sp", ring)
        grad_tokens = finish(sums[-1], low, high)
        out = out.reshape(1, length, heads, HEAD)
        return out, grad_tokens[None]

    return layer


def solution(mesh):
    in_specs = (
        P("fsdp", "sp", None),
        P("fsdp", None, "sp", None),
        P("fsdp", None, "sp", None),
        P("sp", None, None),
        P("sp", None, None),
    )
    out_specs = (P("fsdp", None, "sp", None), P("fsdp", "sp", None))
    shards = make_shards(mesh.shape["fsdp"], mesh.shape["sp"])
    return jax.shard_map(shards, mesh=mesh, in_specs=in_specs, out_specs=out_specs, check_vma=False)
```

profile of v0, /device:TPU:1, one launch (start us, length us, event | category | flops | bytes accessed | tf_op | source)
XLA Modules:
  0.0 134.9 jit_solution(3525332095396886075)
XLA Ops:
  0.6 1.6 %reshape.16.refs_0_ = bf16[192,1536]{1,0:T(8,128)(2,1)S(1)} reshape(bf16[192,3,4,128]{3,2,1,0:T(4,128)(2,1)} %param.6) | data formatting | bytes 1179648 | tf_op jit(solution)/shard_map/reshape | solution.py:430
  2.3 2.7 %collective-permute-start.2 = (bf16[192,1536]{1,0:T(8,128)(2,1)S(1)}, bf16[192,1536]{1,0:T(8,128)(2,1)}, u32[]{:S(2)}, u32[]{:S(2)}) collective-permute-start(bf16[192,1536]{1,0:T(8,128)(2,1)S(1)} %reshape.16.refs_0_), channel_id=1, source_target_pairs={{0,16},{4,20},{8,24},{12,28},{16,0},{20,4},{24,8},{28,12},{1,17},{... | collective-permute-start | bytes 1769480 | tf_op jit(solution)/shard_map/ppermute | solution.py:399
  7.8 2.4 %collective-permute-start.7 = (bf16[128,1536]{1,0:T(8,128)(2,1)S(1)}, bf16[128,1536]{1,0:T(8,128)(2,1)S(1)}, u32[]{:S(2)}, u32[]{:S(2)}) collective-permute-start(bf16[128,1536]{1,0:T(8,128)(2,1)S(1)} %get-tuple-element.25), channel_id=1, source_target_pairs={{0,2},{2,3},{3,1},{1,0},{4,6},{6,7},{7,5},{5,4},{8,10},{10,11},{11... | collective-permute-start | bytes 1179656 | tf_op jit(solution)/shard_map/ppermute | solution.py:435
  11.5 6.4 %collective-permute-done.7.refs_9_ = bf16[128,1536]{1,0:T(8,128)(2,1)S(1)} collective-permute-done((bf16[128,1536]{1,0:T(8,128)(2,1)S(1)}, bf16[128,1536]{1,0:T(8,128)(2,1)S(1)}, u32[]{:S(2)}, u32[]{:S(2)}) %collective-permute-start.7) | collective-permute-done | bytes 393248 | tf_op jit(solution)/shard_map/ppermute | solution.py:435
  17.9 3.1 %collective-permute-start.9 = (bf16[128,1536]{1,0:T(8,128)(2,1)S(1)}, bf16[128,1536]{1,0:T(8,128)(2,1)}, u32[]{:S(2)}, u32[]{:S(2)}) collective-permute-start(bf16[128,1536]{1,0:T(8,128)(2,1)S(1)} %collective-permute-done.7.refs_9_), channel_id=1, source_target_pairs={{0,2},{2,3},{3,1},{1,0},{4,6},{6,7},{7,5},{5,4},{8,10},{10,11},{11... | collective-permute-start | bytes 1179656 | tf_op jit(solution)/shard_map/ppermute | solution.py:435
  21.0 5.3 %collective-permute-done.8.refs_10_ = bf16[128,1536]{1,0:T(8,128)(2,1)S(1)} collective-permute-done((bf16[128,1536]{1,0:T(8,128)(2,1)S(1)}, bf16[128,1536]{1,0:T(8,128)(2,1)S(1)}, u32[]{:S(2)}, u32[]{:S(2)}) %collective-permute-start.8) | collective-permute-done | bytes 393248 | tf_op jit(solution)/shard_map/ppermute | solution.py:435
  26.3 3.1 %collective-permute-start.10 = (bf16[128,1536]{1,0:T(8,128)(2,1)S(1)}, bf16[128,1536]{1,0:T(8,128)(2,1)}, u32[]{:S(2)}, u32[]{:S(2)}) collective-permute-start(bf16[128,1536]{1,0:T(8,128)(2,1)S(1)} %collective-permute-done.8.refs_10_), channel_id=1, source_target_pairs={{0,2},{2,3},{3,1},{1,0},{4,6},{6,7},{7,5},{5,4},{8,10},{10,11},{11... | collective-permute-start | bytes 1179656 | tf_op jit(solution)/shard_map/ppermute | solution.py:435
  34.7 3.2 %collective-permute-start.11 = (bf16[128,1536]{1,0:T(8,128)(2,1)}, bf16[128,1536]{1,0:T(8,128)(2,1)}, u32[]{:S(2)}, u32[]{:S(2)}) collective-permute-start(bf16[128,1536]{1,0:T(8,128)(2,1)} %collective-permute-done.9.refs_11_), channel_id=1, source_target_pairs={{0,2},{2,3},{3,1},{1,0},{4,6},{6,7},{7,5},{5,4},{8,10},{10,11},{11... | collective-permute-start | bytes 1179656 | tf_op jit(solution)/shard_map/ppermute | solution.py:435
  37.9 5.2 %collective-permute-done.10.refs_12_ = bf16[128,1536]{1,0:T(8,128)(2,1)} collective-permute-done((bf16[128,1536]{1,0:T(8,128)(2,1)S(1)}, bf16[128,1536]{1,0:T(8,128)(2,1)}, u32[]{:S(2)}, u32[]{:S(2)}) %collective-permute-start.10) | collective-permute-done | bytes 393248 | tf_op jit(solution)/shard_map/ppermute | solution.py:435
  43.1 3.2 %collective-permute-start.12 = (bf16[128,1536]{1,0:T(8,128)(2,1)}, bf16[128,1536]{1,0:T(8,128)(2,1)}, u32[]{:S(2)}, u32[]{:S(2)}) collective-permute-start(bf16[128,1536]{1,0:T(8,128)(2,1)} %collective-permute-done.10.refs_12_), channel_id=1, source_target_pairs={{0,2},{2,3},{3,1},{1,0},{4,6},{6,7},{7,5},{5,4},{8,10},{10,11},{11... | collective-permute-start | bytes 1179656 | tf_op jit(solution)/shard_map/ppermute | solution.py:435
  47.1 1.4 %copy.11 = bf16[128,8,4,128]{3,1,2,0:T(8,128)(2,1)S(1)} copy(bf16[128,8,4,128]{3,2,1,0:T(4,128)(2,1)} %bitcast.14) | data formatting | bytes 2097152
  48.7 1.5 %pack.1.packed_ref = s32[129]{0:T(256)S(1)} custom-call(s32[128]{0:T(128)S(1)} %reshape.15.code_ref, bf16[1024,512]{1,0:T(8,128)(2,1)S(1)} %bitcast.11), custom_call_target="tpu_custom_call" | custom-call | tf_op jit(solution)/shard_map/pack/pallas_call | solution.py:364
  50.2 4.4 %collective-permute-done.6.refs_7_ = bf16[192,1536]{1,0:T(8,128)(2,1)} collective-permute-done((bf16[192,1536]{1,0:T(8,128)(2,1)}, bf16[192,1536]{1,0:T(8,128)(2,1)}, u32[]{:S(2)}, u32[]{:S(2)}) %collective-permute-start.6) | collective-permute-done | bytes 589856 | tf_op jit(solution)/shard_map/ppermute | solution.py:399
  56.7 5.9 %project.1 = (bf16[1536,1536]{1,0:T(8,128)(2,1)S(1)}, bf16[768,1536]{1,0:T(8,128)(2,1)S(1)}) custom-call(bf16[192,1536]{1,0:T(8,128)(2,1)S(1)} %reshape.16.refs_0_, bf16[192,1536]{1,0:T(8,128)(2,1)S(1)} %collective-permute-done.refs_1_, bf16[192,1536]{1,0:T(8,128)(2,1)S(1)} %copy-done.2, bf16[192,1536]{1,0:T(8,128)(2,1)} %collective-permute-done.2.refs_3_, ...), custom_call_target="tpu_custom_call" | custom-call | flops 3623878656 | bytes 14155776 | tf_op jit(solution)/shard_map/project/pallas_call | solution.py:65
  62.6 14.3 %attention.1 = (bf16[1024,512]{1,0:T(8,128)(2,1)S(1)}, bf16[1024,1536]{1,0:T(8,128)(2,1)S(1)}, bf16[128,1536]{1,0:T(8,128)(2,1)S(1)}, bf16[128,1536]{1,0:T(8,128)(2,1)S(1)}) custom-call(s32[129]{0:T(256)S(1)} %pack.1.packed_ref, bf16[768,1536]{1,0:T(8,128)(2,1)S(1)} %get-tuple-element.13.early_ref, bf16[128,1536]{1,0:T(8,128)(2,1)} %collective-permute-done.11.late_ref, ...), custom_call_target="tpu_custom_call" | custom-call | flops 3221225472 | bytes 8388608 | tf_op jit(solution)/shard_map/attention/pallas_call | solution.py:313
  78.4 3.8 %products.1 = (f32[128,1536]{1,0:T(8,128)S(1)}, f32[128,1536]{1,0:T(8,128)S(1)}, f32[128,1536]{1,0:T(8,128)S(1)}, f32[128,1536]{1,0:T(8,128)S(1)}, f32[256,1536]{1,0:T(8,128)S(1)}) custom-call(bf16[1024,1536]{1,0:T(8,128)(2,1)S(1)} %get-tuple-element.16.dqkv_ref, bf16[1536,1536]{1,0:T(8,128)(2,1)S(1)} %get-tuple-element.14.w_ref), custom_call_target="tpu_custom_call" | custom-call | flops 3623878656 | bytes 11796480 | tf_op jit(solution)/shard_map/products/pallas_call | solution.py:100
  83.7 1.6 %collective-permute-start.17 = (bf16[128,1536]{1,0:T(8,128)(2,1)S(1)}, bf16[128,1536]{1,0:T(8,128)(2,1)S(1)}, u32[]{:S(2)}, u32[]{:S(2)}) collective-permute-start(bf16[128,1536]{1,0:T(8,128)(2,1)S(1)} %add_convert_fusion.1), channel_id=1, source_target_pairs={{0,2},{2,3},{3,1},{1,0},{4,6},{6,7},{7,5},{5,4},{8,10},{10,11},{11... | collective-permute-start | bytes 1179656 | tf_op jit(solution)/shard_map/ppermute | solution.py:449
  85.2 6.8 %collective-permute-done.13 = bf16[128,1536]{1,0:T(8,128)(2,1)S(1)} collective-permute-done((bf16[128,1536]{1,0:T(8,128)(2,1)S(1)}, bf16[128,1536]{1,0:T(8,128)(2,1)S(1)}, u32[]{:S(2)}, u32[]{:S(2)}) %collective-permute-start.13) | collective-permute-done | bytes 393248 | tf_op jit(solution)/shard_map/ppermute | solution.py:446
  92.1 1.7 %collective-permute-start.14 = (bf16[128,1536]{1,0:T(8,128)(2,1)S(1)}, bf16[128,1536]{1,0:T(8,128)(2,1)S(1)}, u32[]{:S(2)}, u32[]{:S(2)}) collective-permute-start(bf16[128,1536]{1,0:T(8,128)(2,1)S(1)} %add_convert_fusion.3), channel_id=1, source_target_pairs={{0,2},{2,3},{3,1},{1,0},{4,6},{6,7},{7,5},{5,4},{8,10},{10,11},{11... | collective-permute-start | bytes 1179656 | tf_op jit(solution)/shard_map/ppermute | solution.py:446
  93.8 6.7 %collective-permute-done.17 = bf16[128,1536]{1,0:T(8,128)(2,1)S(1)} collective-permute-done((bf16[128,1536]{1,0:T(8,128)(2,1)S(1)}, bf16[128,1536]{1,0:T(8,128)(2,1)S(1)}, u32[]{:S(2)}, u32[]{:S(2)}) %collective-permute-start.17) | collective-permute-done | bytes 393248 | tf_op jit(solution)/shard_map/ppermute | solution.py:449
  101.3 1.6 %collective-permute-start.18 = (bf16[128,1536]{1,0:T(8,128)(2,1)}, bf16[128,1536]{1,0:T(8,128)(2,1)S(1)}, u32[]{:S(2)}, u32[]{:S(2)}) collective-permute-start(bf16[128,1536]{1,0:T(8,128)(2,1)} %add_convert_fusion), channel_id=1, source_target_pairs={{0,2},{2,3},{3,1},{1,0},{4,6},{6,7},{7,5},{5,4},{8,10},{10,11},{11... | collective-permute-start | bytes 1179656 | tf_op jit(solution)/shard_map/ppermute | solution.py:449
  102.9 6.0 %collective-permute-done.14 = bf16[128,1536]{1,0:T(8,128)(2,1)S(1)} collective-permute-done((bf16[128,1536]{1,0:T(8,128)(2,1)S(1)}, bf16[128,1536]{1,0:T(8,128)(2,1)S(1)}, u32[]{:S(2)}, u32[]{:S(2)}) %collective-permute-start.14) | collective-permute-done | bytes 393248 | tf_op jit(solution)/shard_map/ppermute | solution.py:446
  109.7 1.6 %collective-permute-start.15 = (bf16[128,1536]{1,0:T(8,128)(2,1)}, bf16[128,1536]{1,0:T(8,128)(2,1)S(1)}, u32[]{:S(2)}, u32[]{:S(2)}) collective-permute-start(bf16[128,1536]{1,0:T(8,128)(2,1)} %add_convert_fusion.2), channel_id=1, source_target_pairs={{0,2},{2,3},{3,1},{1,0},{4,6},{6,7},{7,5},{5,4},{8,10},{10,11},{11... | collective-permute-start | bytes 1179656 | tf_op jit(solution)/shard_map/ppermute | solution.py:446
  111.3 21.4 %stagger.1 = s32[1]{0:T(128)} custom-call(), custom_call_target="tpu_custom_call" | custom-call | tf_op jit(solution)/shard_map/stagger/pallas_call | solution.py:380
  (41 shorter events, 19.2 us)
Async XLA Ops:
  0.6 54.0 %copy-start = (bf16[1,256,1536]{2,1,0:T(8,128)(2,1)S(1)}, bf16[1,256,1536]{2,1,0:T(8,128)(2,1)}, u32[]{:S(2)}) copy-start(bf16[1,256,1536]{2,1,0:T(8,128)(2,1)} %param.5) | copy-start | bytes 2359300
  2.2 4.0 %collective-permute-start = (bf16[192,1536]{1,0:T(8,128)(2,1)S(1)}, bf16[192,1536]{1,0:T(8,128)(2,1)S(1)}, u32[]{:S(2)}, u32[]{:S(2)}) collective-permute-start(bf16[192,1536]{1,0:T(8,128)(2,1)S(1)} %reshape.16.refs_0_), channel_id=1, source_target_pairs={{0,4},{4,0},{8,12},{12,8},{16,20},{20,16},{24,28},{28,24},{1,5},{5... | collective-permute-start | bytes 1769480 | tf_op jit(solution)/shard_map/ppermute | solution.py:399
  2.3 27.8 %collective-permute-start.2 = (bf16[192,1536]{1,0:T(8,128)(2,1)S(1)}, bf16[192,1536]{1,0:T(8,128)(2,1)}, u32[]{:S(2)}, u32[]{:S(2)}) collective-permute-start(bf16[192,1536]{1,0:T(8,128)(2,1)S(1)} %reshape.16.refs_0_), channel_id=1, source_target_pairs={{0,16},{4,20},{8,24},{12,28},{16,0},{20,4},{24,8},{28,12},{1,17},{... | collective-permute-start | bytes 1769480 | tf_op jit(solution)/shard_map/ppermute | solution.py:399
  5.0 26.5 %collective-permute-start.1 = (bf16[192,1536]{1,0:T(8,128)(2,1)S(1)}, bf16[192,1536]{1,0:T(8,128)(2,1)S(1)}, u32[]{:S(2)}, u32[]{:S(2)}) collective-permute-start(bf16[192,1536]{1,0:T(8,128)(2,1)S(1)} %reshape.16.refs_0_), channel_id=1, source_target_pairs={{0,8},{4,12},{8,0},{12,4},{16,24},{20,28},{24,16},{28,20},{1,9},{5... | collective-permute-start | bytes 1769480 | tf_op jit(solution)/shard_map/ppermute | solution.py:399
  6.3 26.3 %collective-permute-start.3 = (bf16[192,1536]{1,0:T(8,128)(2,1)S(1)}, bf16[192,1536]{1,0:T(8,128)(2,1)}, u32[]{:S(2)}, u32[]{:S(2)}) collective-permute-start(bf16[192,1536]{1,0:T(8,128)(2,1)S(1)} %collective-permute-done.refs_1_), channel_id=1, source_target_pairs={{0,8},{4,12},{8,0},{12,4},{16,24},{20,28},{24,16},{28,20},{1,9},{5... | collective-permute-start | bytes 1769480 | tf_op jit(solution)/shard_map/ppermute | solution.py:399
  7.8 10.0 %collective-permute-start.7 = (bf16[128,1536]{1,0:T(8,128)(2,1)S(1)}, bf16[128,1536]{1,0:T(8,128)(2,1)S(1)}, u32[]{:S(2)}, u32[]{:S(2)}) collective-permute-start(bf16[128,1536]{1,0:T(8,128)(2,1)S(1)} %get-tuple-element.25), channel_id=1, source_target_pairs={{0,2},{2,3},{3,1},{1,0},{4,6},{6,7},{7,5},{5,4},{8,10},{10,11},{11... | collective-permute-start | bytes 1179656 | tf_op jit(solution)/shard_map/ppermute | solution.py:435
  10.2 16.1 %collective-permute-start.8 = (bf16[128,1536]{1,0:T(8,128)(2,1)S(1)}, bf16[128,1536]{1,0:T(8,128)(2,1)S(1)}, u32[]{:S(2)}, u32[]{:S(2)}) collective-permute-start(bf16[128,1536]{1,0:T(8,128)(2,1)S(1)} %get-tuple-element.24), channel_id=1, source_target_pairs={{0,2},{2,3},{3,1},{1,0},{4,6},{6,7},{7,5},{5,4},{8,10},{10,11},{11... | collective-permute-start | bytes 1179656 | tf_op jit(solution)/shard_map/ppermute | solution.py:435
  17.9 16.9 %collective-permute-start.9 = (bf16[128,1536]{1,0:T(8,128)(2,1)S(1)}, bf16[128,1536]{1,0:T(8,128)(2,1)}, u32[]{:S(2)}, u32[]{:S(2)}) collective-permute-start(bf16[128,1536]{1,0:T(8,128)(2,1)S(1)} %collective-permute-done.7.refs_9_), channel_id=1, source_target_pairs={{0,2},{2,3},{3,1},{1,0},{4,6},{6,7},{7,5},{5,4},{8,10},{10,11},{11... | collective-permute-start | bytes 1179656 | tf_op jit(solution)/shard_map/ppermute | solution.py:435
  26.3 16.9 %collective-permute-start.10 = (bf16[128,1536]{1,0:T(8,128)(2,1)S(1)}, bf16[128,1536]{1,0:T(8,128)(2,1)}, u32[]{:S(2)}, u32[]{:S(2)}) collective-permute-start(bf16[128,1536]{1,0:T(8,128)(2,1)S(1)} %collective-permute-done.8.refs_10_), channel_id=1, source_target_pairs={{0,2},{2,3},{3,1},{1,0},{4,6},{6,7},{7,5},{5,4},{8,10},{10,11},{11... | collective-permute-start | bytes 1179656 | tf_op jit(solution)/shard_map/ppermute | solution.py:435
  29.4 0.7 copy-start.3
  30.1 20.0 %collective-permute-start.4 = (bf16[192,1536]{1,0:T(8,128)(2,1)S(1)}, bf16[192,1536]{1,0:T(8,128)(2,1)}, u32[]{:S(2)}, u32[]{:S(2)}) collective-permute-start(bf16[192,1536]{1,0:T(8,128)(2,1)S(1)} %collective-permute-done.refs_1_), channel_id=1, source_target_pairs={{0,16},{4,20},{8,24},{12,28},{16,0},{20,4},{24,8},{28,12},{1,17},{... | collective-permute-start | bytes 1769480 | tf_op jit(solution)/shard_map/ppermute | solution.py:399
  31.5 0.8 copy-start.1
  32.3 17.9 %collective-permute-start.5 = (bf16[192,1536]{1,0:T(8,128)(2,1)}, bf16[192,1536]{1,0:T(8,128)(2,1)}, u32[]{:S(2)}, u32[]{:S(2)}) collective-permute-start(bf16[192,1536]{1,0:T(8,128)(2,1)} %collective-permute-done.2.refs_3_), channel_id=1, source_target_pairs={{0,8},{4,12},{8,0},{12,4},{16,24},{20,28},{24,16},{28,20},{1,9},{5... | collective-permute-start | bytes 1769480 | tf_op jit(solution)/shard_map/ppermute | solution.py:399
  32.5 22.1 %collective-permute-start.6 = (bf16[192,1536]{1,0:T(8,128)(2,1)}, bf16[192,1536]{1,0:T(8,128)(2,1)}, u32[]{:S(2)}, u32[]{:S(2)}) collective-permute-start(bf16[192,1536]{1,0:T(8,128)(2,1)} %collective-permute-done.3.refs_4_), channel_id=1, source_target_pairs={{0,16},{4,20},{8,24},{12,28},{16,0},{20,4},{24,8},{28,12},{1,17},{... | collective-permute-start | bytes 1769480 | tf_op jit(solution)/shard_map/ppermute | solution.py:399
  34.7 27.9 %collective-permute-start.11 = (bf16[128,1536]{1,0:T(8,128)(2,1)}, bf16[128,1536]{1,0:T(8,128)(2,1)}, u32[]{:S(2)}, u32[]{:S(2)}) collective-permute-start(bf16[128,1536]{1,0:T(8,128)(2,1)} %collective-permute-done.9.refs_11_), channel_id=1, source_target_pairs={{0,2},{2,3},{3,1},{1,0},{4,6},{6,7},{7,5},{5,4},{8,10},{10,11},{11... | collective-permute-start | bytes 1179656 | tf_op jit(solution)/shard_map/ppermute | solution.py:435
  43.1 19.5 %collective-permute-start.12 = (bf16[128,1536]{1,0:T(8,128)(2,1)}, bf16[128,1536]{1,0:T(8,128)(2,1)}, u32[]{:S(2)}, u32[]{:S(2)}) collective-permute-start(bf16[128,1536]{1,0:T(8,128)(2,1)} %collective-permute-done.10.refs_12_), channel_id=1, source_target_pairs={{0,2},{2,3},{3,1},{1,0},{4,6},{6,7},{7,5},{5,4},{8,10},{10,11},{11... | collective-permute-start | bytes 1179656 | tf_op jit(solution)/shard_map/ppermute | solution.py:435
  54.6 1.1 copy-start.2
  55.7 1.0 copy-start.4
  76.9 6.7 %collective-permute-start.16 = (bf16[128,1536]{1,0:T(8,128)(2,1)S(1)}, bf16[128,1536]{1,0:T(8,128)(2,1)S(1)}, u32[]{:S(2)}, u32[]{:S(2)}) collective-permute-start(bf16[128,1536]{1,0:T(8,128)(2,1)S(1)} %get-tuple-element.23), channel_id=1, source_target_pairs={{0,2},{2,3},{3,1},{1,0},{4,6},{6,7},{7,5},{5,4},{8,10},{10,11},{11... | collective-permute-start | bytes 1179656 | tf_op jit(solution)/shard_map/ppermute | solution.py:449
  77.6 14.5 %collective-permute-start.13 = (bf16[128,1536]{1,0:T(8,128)(2,1)S(1)}, bf16[128,1536]{1,0:T(8,128)(2,1)S(1)}, u32[]{:S(2)}, u32[]{:S(2)}) collective-permute-start(bf16[128,1536]{1,0:T(8,128)(2,1)S(1)} %get-tuple-element.20), channel_id=1, source_target_pairs={{0,2},{2,3},{3,1},{1,0},{4,6},{6,7},{7,5},{5,4},{8,10},{10,11},{11... | collective-permute-start | bytes 1179656 | tf_op jit(solution)/shard_map/ppermute | solution.py:446
  83.7 16.8 %collective-permute-start.17 = (bf16[128,1536]{1,0:T(8,128)(2,1)S(1)}, bf16[128,1536]{1,0:T(8,128)(2,1)S(1)}, u32[]{:S(2)}, u32[]{:S(2)}) collective-permute-start(bf16[128,1536]{1,0:T(8,128)(2,1)S(1)} %add_convert_fusion.1), channel_id=1, source_target_pairs={{0,2},{2,3},{3,1},{1,0},{4,6},{6,7},{7,5},{5,4},{8,10},{10,11},{11... | collective-permute-start | bytes 1179656 | tf_op jit(solution)/shard_map/ppermute | solution.py:449
  92.1 16.8 %collective-permute-start.14 = (bf16[128,1536]{1,0:T(8,128)(2,1)S(1)}, bf16[128,1536]{1,0:T(8,128)(2,1)S(1)}, u32[]{:S(2)}, u32[]{:S(2)}) collective-permute-start(bf16[128,1536]{1,0:T(8,128)(2,1)S(1)} %add_convert_fusion.3), channel_id=1, source_target_pairs={{0,2},{2,3},{3,1},{1,0},{4,6},{6,7},{7,5},{5,4},{8,10},{10,11},{11... | collective-permute-start | bytes 1179656 | tf_op jit(solution)/shard_map/ppermute | solution.py:446
  101.3 32.6 %collective-permute-start.18 = (bf16[128,1536]{1,0:T(8,128)(2,1)}, bf16[128,1536]{1,0:T(8,128)(2,1)S(1)}, u32[]{:S(2)}, u32[]{:S(2)}) collective-permute-start(bf16[128,1536]{1,0:T(8,128)(2,1)} %add_convert_fusion), channel_id=1, source_target_pairs={{0,2},{2,3},{3,1},{1,0},{4,6},{6,7},{7,5},{5,4},{8,10},{10,11},{11... | collective-permute-start | bytes 1179656 | tf_op jit(solution)/shard_map/ppermute | solution.py:449
  109.7 24.1 %collective-permute-start.15 = (bf16[128,1536]{1,0:T(8,128)(2,1)}, bf16[128,1536]{1,0:T(8,128)(2,1)S(1)}, u32[]{:S(2)}, u32[]{:S(2)}) collective-permute-start(bf16[128,1536]{1,0:T(8,128)(2,1)} %add_convert_fusion.2), channel_id=1, source_target_pairs={{0,2},{2,3},{3,1},{1,0},{4,6},{6,7},{7,5},{5,4},{8,10},{10,11},{11... | collective-permute-start | bytes 1179656 | tf_op jit(solution)/shard_map/ppermute | solution.py:446
where the time goes:
time: 135 us
  Pallas kernels  48 us (36%)
  waiting for transfers between devices  43.6 us (32%)
  starting transfers between devices  31 us (23%)
  local copies, waits for them, and re-layouts  9.11 us (7%)
  other arithmetic  2.5 us (2%)
    pallas_call x1, Pallas kernels, stagger(): pl.pallas_call(stagger_kernel, out_shape=jax.ShapeDtypeStruct((1,), jnp.i...  21.4 us
    ppermute x6, waiting for transfers between devices, layer(): halves[side] = lax.ppermute(halves[side], 'sp', ring)  18.3 us
    ppermute x6, starting transfers between devices, layer(): halves[side] = lax.ppermute(halves[side], 'sp', ring)  16.3 us
    pallas_call x1, Pallas kernels, attention(): pl.pallas_call(functools.partial(attention_kernel, heads=heads, all_slots...  14.3 us
    ppermute x3, waiting for transfers between devices, layer(): low = lax.ppermute(low, 'sp', ring)  12.8 us
    ppermute x3, waiting for transfers between devices, layer(): high = lax.ppermute(high, 'sp', ring)  8.06 us
    ppermute x7, starting transfers between devices, swap(): return lax.ppermute(value, axis, [(i, i ^ bit) for i in range(count)])  6.81 us
    pallas_call x1, Pallas kernels, project(): pl.pallas_call(functools.partial(project_kernel, keys=tuple(keys), parts=...  5.94 us
  transfers between devices with their start and end apart: 19, of which 9 were waited for; matrix products, arithmetic and copies ran while one was open for 5% of the time, Pallas kernels for 24%

commit v1 on v0

--- a/solution.py
+++ b/solution.py
@@ -108,6 +108,20 @@
         ),
         compiler_params=pltpu.CompilerParams(vmem_limit_bytes=4 << 20),
     )(dqkv, w)
+
+
+def join_kernel(own_ref, arrived_ref, out_ref):
+    out_ref[...] = (own_ref[...] + arrived_ref[...].astype(jnp.float32)).astype(jnp.bfloat16)
+
+
+def join(own, arrived):
+    return pl.pallas_call(
+        join_kernel,
+        out_shape=jax.ShapeDtypeStruct(own.shape, jnp.bfloat16),
+        out_specs=pl.BlockSpec(memory_space=pltpu.VMEM),
+        name="join",
+        compiler_params=pltpu.CompilerParams(vmem_limit_bytes=1 << 20),
+    )(own, arrived)
 
 
 def finish_kernel(own_ref, low_ref, high_ref, out_ref):
@@ -337,7 +351,7 @@
             bytes_accessed=16 * length * width,
             transcendentals=heads * tile_count * slots * TILE * TILE,
         ),
-        compiler_params=pltpu.CompilerParams(vmem_limit_bytes=18 << 20),
+        compiler_params=pltpu.CompilerParams(vmem_limit_bytes=14 << 20),
     )(codes, early, late, last, w, dout)
 
 
@@ -442,10 +456,10 @@
         sums = products(dqkv, w, 2 * chunk, [half] * (2 * sp_count - 4) + [chunk])
         for step in range(1, sp_count):
             if step > 1:
-                low = (sums[2 * step - 4] + low.astype(jnp.float32)).astype(jnp.bfloat16)
+                low = join(sums[2 * step - 4], low)
             low = lax.ppermute(low, "sp", ring)
             if step > 1:
-                high = (sums[2 * step - 3] + high.astype(jnp.float32)).astype(jnp.bfloat16)
+                high = join(sums[2 * step - 3], high)
             high = lax.ppermute(high, "sp", ring)
         grad_tokens = finish(sums[-1], low, high)
         out = out.reshape(1, length, heads, HEAD)

time: 135 us -> 135 us (level)
  Pallas kernels: 48 us -> 49.9 us
  other arithmetic: 2.5 us -> 0.72 us
    convert_element_type x4 -> x0, other arithmetic: 1.78 us -> none  [the longest x2 0.9 us: layer(): low = (sums[2 * step - 4] + low.astype(jnp.float32)).astype(jnp.bfloat16)]
    pallas_call x0 -> x4, Pallas kernels: none -> 1.76 us  [join(): pl.pallas_call(join_kernel, out_shape=jax.ShapeDtypeStruct(own.shape, jnp...]
  transfers between devices with their start and end apart: 19 -> 19, of which waited for: 9 -> 9; matrix products, arithmetic and copies ran while one was open for 5% -> 3% of each run, Pallas kernels for 24% -> 26%
where the time goes in v1:
time: 135 us
  Pallas kernels  49.9 us (37%)
  waiting for transfers between devices  43.5 us (32%)
  starting transfers between devices  30.9 us (23%)
  local copies, waits for them, and re-layouts  9.11 us (7%)
    pallas_call x1, Pallas kernels, stagger(): pl.pallas_call(stagger_kernel, out_shape=jax.ShapeDtypeStruct((1,), jnp.i...  21.4 us
    ppermute x6, waiting for transfers between devices, layer(): halves[side] = lax.ppermute(halves[side], 'sp', ring)  18.3 us
    ppermute x6, starting transfers between devices, layer(): halves[side] = lax.ppermute(halves[side], 'sp', ring)  16.3 us
    pallas_call x1, Pallas kernels, attention(): pl.pallas_call(functools.partial(attention_kernel, heads=heads, all_slots...  14.4 us
    ppermute x3, waiting for transfers between devices, layer(): low = lax.ppermute(low, 'sp', ring)  12.8 us
    ppermute x3, waiting for transfers between devices, layer(): high = lax.ppermute(high, 'sp', ring)  8 us
    ppermute x7, starting transfers between devices, swap(): return lax.ppermute(value, axis, [(i, i ^ bit) for i in range(count)])  6.81 us
    pallas_call x1, Pallas kernels, project(): pl.pallas_call(functools.partial(project_kernel, keys=tuple(keys), parts=...  5.94 us
  transfers between devices with their start and end apart: 19, of which 9 were waited for; matrix products, arithmetic and copies ran while one was open for 3% of the time, Pallas kernels for 26%

profile of v1, /device:TPU:1, one launch (start us, length us, event | category | flops | bytes accessed | tf_op | source)
XLA Modules:
  0.0 135.0 jit_solution(5682476097324959044)
XLA Ops:
  0.6 1.6 %reshape.16.refs_0_ = bf16[192,1536]{1,0:T(8,128)(2,1)S(1)} reshape(bf16[192,3,4,128]{3,2,1,0:T(4,128)(2,1)} %param.6) | data formatting | bytes 1179648 | tf_op jit(solution)/shard_map/reshape | solution.py:444
  2.3 2.7 %collective-permute-start.2 = (bf16[192,1536]{1,0:T(8,128)(2,1)S(1)}, bf16[192,1536]{1,0:T(8,128)(2,1)}, u32[]{:S(2)}, u32[]{:S(2)}) collective-permute-start(bf16[192,1536]{1,0:T(8,128)(2,1)S(1)} %reshape.16.refs_0_), channel_id=1, source_target_pairs={{0,16},{4,20},{8,24},{12,28},{16,0},{20,4},{24,8},{28,12},{1,17},{... | collective-permute-start | bytes 1769480 | tf_op jit(solution)/shard_map/ppermute | solution.py:413
  7.8 2.4 %collective-permute-start.7 = (bf16[128,1536]{1,0:T(8,128)(2,1)S(1)}, bf16[128,1536]{1,0:T(8,128)(2,1)S(1)}, u32[]{:S(2)}, u32[]{:S(2)}) collective-permute-start(bf16[128,1536]{1,0:T(8,128)(2,1)S(1)} %get-tuple-element.25), channel_id=1, source_target_pairs={{0,2},{2,3},{3,1},{1,0},{4,6},{6,7},{7,5},{5,4},{8,10},{10,11},{11... | collective-permute-start | bytes 1179656 | tf_op jit(solution)/shard_map/ppermute | solution.py:449
  11.5 6.4 %collective-permute-done.7.refs_9_ = bf16[128,1536]{1,0:T(8,128)(2,1)S(1)} collective-permute-done((bf16[128,1536]{1,0:T(8,128)(2,1)S(1)}, bf16[128,1536]{1,0:T(8,128)(2,1)S(1)}, u32[]{:S(2)}, u32[]{:S(2)}) %collective-permute-start.7) | collective-permute-done | bytes 393248 | tf_op jit(solution)/shard_map/ppermute | solution.py:449
  17.9 3.1 %collective-permute-start.9 = (bf16[128,1536]{1,0:T(8,128)(2,1)S(1)}, bf16[128,1536]{1,0:T(8,128)(2,1)}, u32[]{:S(2)}, u32[]{:S(2)}) collective-permute-start(bf16[128,1536]{1,0:T(8,128)(2,1)S(1)} %collective-permute-done.7.refs_9_), channel_id=1, source_target_pairs={{0,2},{2,3},{3,1},{1,0},{4,6},{6,7},{7,5},{5,4},{8,10},{10,11},{11... | collective-permute-start | bytes 1179656 | tf_op jit(solution)/shard_map/ppermute | solution.py:449
  21.0 5.3 %collective-permute-done.8.refs_10_ = bf16[128,1536]{1,0:T(8,128)(2,1)S(1)} collective-permute-done((bf16[128,1536]{1,0:T(8,128)(2,1)S(1)}, bf16[128,1536]{1,0:T(8,128)(2,1)S(1)}, u32[]{:S(2)}, u32[]{:S(2)}) %collective-permute-start.8) | collective-permute-done | bytes 393248 | tf_op jit(solution)/shard_map/ppermute | solution.py:449
  26.3 3.1 %collective-permute-start.10 = (bf16[128,1536]{1,0:T(8,128)(2,1)S(1)}, bf16[128,1536]{1,0:T(8,128)(2,1)}, u32[]{:S(2)}, u32[]{:S(2)}) collective-permute-start(bf16[128,1536]{1,0:T(8,128)(2,1)S(1)} %collective-permute-done.8.refs_10_), channel_id=1, source_target_pairs={{0,2},{2,3},{3,1},{1,0},{4,6},{6,7},{7,5},{5,4},{8,10},{10,11},{11... | collective-permute-start | bytes 1179656 | tf_op jit(solution)/shard_map/ppermute | solution.py:449
  34.7 3.2 %collective-permute-start.11 = (bf16[128,1536]{1,0:T(8,128)(2,1)}, bf16[128,1536]{1,0:T(8,128)(2,1)}, u32[]{:S(2)}, u32[]{:S(2)}) collective-permute-start(bf16[128,1536]{1,0:T(8,128)(2,1)} %collective-permute-done.9.refs_11_), channel_id=1, source_target_pairs={{0,2},{2,3},{3,1},{1,0},{4,6},{6,7},{7,5},{5,4},{8,10},{10,11},{11... | collective-permute-start | bytes 1179656 | tf_op jit(solution)/shard_map/ppermute | solution.py:449
  37.9 5.2 %collective-permute-done.10.refs_12_ = bf16[128,1536]{1,0:T(8,128)(2,1)} collective-permute-done((bf16[128,1536]{1,0:T(8,128)(2,1)S(1)}, bf16[128,1536]{1,0:T(8,128)(2,1)}, u32[]{:S(2)}, u32[]{:S(2)}) %collective-permute-start.10) | collective-permute-done | bytes 393248 | tf_op jit(solution)/shard_map/ppermute | solution.py:449
  43.1 3.2 %collective-permute-start.12 = (bf16[128,1536]{1,0:T(8,128)(2,1)}, bf16[128,1536]{1,0:T(8,128)(2,1)}, u32[]{:S(2)}, u32[]{:S(2)}) collective-permute-start(bf16[128,1536]{1,0:T(8,128)(2,1)} %collective-permute-done.10.refs_12_), channel_id=1, source_target_pairs={{0,2},{2,3},{3,1},{1,0},{4,6},{6,7},{7,5},{5,4},{8,10},{10,11},{11... | collective-permute-start | bytes 1179656 | tf_op jit(solution)/shard_map/ppermute | solution.py:449
  47.1 1.4 %copy.11 = bf16[128,8,4,128]{3,1,2,0:T(8,128)(2,1)S(1)} copy(bf16[128,8,4,128]{3,2,1,0:T(4,128)(2,1)} %bitcast.14) | data formatting | bytes 2097152
  48.7 1.5 %pack.1.packed_ref = s32[129]{0:T(256)S(1)} custom-call(s32[128]{0:T(128)S(1)} %reshape.15.code_ref, bf16[1024,512]{1,0:T(8,128)(2,1)S(1)} %bitcast.11), custom_call_target="tpu_custom_call" | custom-call | tf_op jit(solution)/shard_map/pack/pallas_call | solution.py:378
  50.2 4.4 %collective-permute-done.6.refs_7_ = bf16[192,1536]{1,0:T(8,128)(2,1)} collective-permute-done((bf16[192,1536]{1,0:T(8,128)(2,1)}, bf16[192,1536]{1,0:T(8,128)(2,1)}, u32[]{:S(2)}, u32[]{:S(2)}) %collective-permute-start.6) | collective-permute-done | bytes 589856 | tf_op jit(solution)/shard_map/ppermute | solution.py:413
  56.7 5.9 %project.1 = (bf16[1536,1536]{1,0:T(8,128)(2,1)S(1)}, bf16[768,1536]{1,0:T(8,128)(2,1)S(1)}) custom-call(bf16[192,1536]{1,0:T(8,128)(2,1)S(1)} %reshape.16.refs_0_, bf16[192,1536]{1,0:T(8,128)(2,1)S(1)} %collective-permute-done.refs_1_, bf16[192,1536]{1,0:T(8,128)(2,1)S(1)} %copy-done.2, bf16[192,1536]{1,0:T(8,128)(2,1)} %collective-permute-done.2.refs_3_, ...), custom_call_target="tpu_custom_call" | custom-call | flops 3623878656 | bytes 14155776 | tf_op jit(solution)/shard_map/project/pallas_call | solution.py:65
  62.6 14.4 %attention.1 = (bf16[1024,512]{1,0:T(8,128)(2,1)S(1)}, bf16[1024,1536]{1,0:T(8,128)(2,1)S(1)}, bf16[128,1536]{1,0:T(8,128)(2,1)S(1)}, bf16[128,1536]{1,0:T(8,128)(2,1)S(1)}) custom-call(s32[129]{0:T(256)S(1)} %pack.1.packed_ref, bf16[768,1536]{1,0:T(8,128)(2,1)S(1)} %get-tuple-element.13.early_ref, bf16[128,1536]{1,0:T(8,128)(2,1)} %collective-permute-done.11.late_ref, ...), custom_call_target="tpu_custom_call" | custom-call | flops 3221225472 | bytes 8388608 | tf_op jit(solution)/shard_map/attention/pallas_call | solution.py:327
  78.5 3.9 %products.1 = (f32[128,1536]{1,0:T(8,128)S(1)}, f32[128,1536]{1,0:T(8,128)S(1)}, f32[128,1536]{1,0:T(8,128)S(1)}, f32[128,1536]{1,0:T(8,128)S(1)}, f32[256,1536]{1,0:T(8,128)S(1)}) custom-call(bf16[1024,1536]{1,0:T(8,128)(2,1)S(1)} %get-tuple-element.16.dqkv_ref, bf16[1536,1536]{1,0:T(8,128)(2,1)S(1)} %get-tuple-element.14.w_ref), custom_call_target="tpu_custom_call" | custom-call | flops 3623878656 | bytes 11796480 | tf_op jit(solution)/shard_map/products/pallas_call | solution.py:100
  83.8 1.6 %collective-permute-start.17 = (bf16[128,1536]{1,0:T(8,128)(2,1)S(1)}, bf16[128,1536]{1,0:T(8,128)(2,1)S(1)}, u32[]{:S(2)}, u32[]{:S(2)}) collective-permute-start(bf16[128,1536]{1,0:T(8,128)(2,1)S(1)} %join.6), channel_id=1, source_target_pairs={{0,2},{2,3},{3,1},{1,0},{4,6},{6,7},{7,5},{5,4},{8,10},{10,11},{11... | collective-permute-start | bytes 1179656 | tf_op jit(solution)/shard_map/ppermute | solution.py:463
  85.3 6.8 %collective-permute-done.13.arrived_ref = bf16[128,1536]{1,0:T(8,128)(2,1)S(1)} collective-permute-done((bf16[128,1536]{1,0:T(8,128)(2,1)S(1)}, bf16[128,1536]{1,0:T(8,128)(2,1)S(1)}, u32[]{:S(2)}, u32[]{:S(2)}) %collective-permute-start.13) | collective-permute-done | bytes 393248 | tf_op jit(solution)/shard_map/ppermute | solution.py:460
  92.2 1.7 %collective-permute-start.14 = (bf16[128,1536]{1,0:T(8,128)(2,1)S(1)}, bf16[128,1536]{1,0:T(8,128)(2,1)S(1)}, u32[]{:S(2)}, u32[]{:S(2)}) collective-permute-start(bf16[128,1536]{1,0:T(8,128)(2,1)S(1)} %join.4), channel_id=1, source_target_pairs={{0,2},{2,3},{3,1},{1,0},{4,6},{6,7},{7,5},{5,4},{8,10},{10,11},{11... | collective-permute-start | bytes 1179656 | tf_op jit(solution)/shard_map/ppermute | solution.py:460
  93.9 6.7 %collective-permute-done.17.arrived_ref = bf16[128,1536]{1,0:T(8,128)(2,1)S(1)} collective-permute-done((bf16[128,1536]{1,0:T(8,128)(2,1)S(1)}, bf16[128,1536]{1,0:T(8,128)(2,1)S(1)}, u32[]{:S(2)}, u32[]{:S(2)}) %collective-permute-start.17) | collective-permute-done | bytes 393248 | tf_op jit(solution)/shard_map/ppermute | solution.py:463
  101.4 1.6 %collective-permute-start.18 = (bf16[128,1536]{1,0:T(8,128)(2,1)}, bf16[128,1536]{1,0:T(8,128)(2,1)S(1)}, u32[]{:S(2)}, u32[]{:S(2)}) collective-permute-start(bf16[128,1536]{1,0:T(8,128)(2,1)} %join.7), channel_id=1, source_target_pairs={{0,2},{2,3},{3,1},{1,0},{4,6},{6,7},{7,5},{5,4},{8,10},{10,11},{11... | collective-permute-start | bytes 1179656 | tf_op jit(solution)/shard_map/ppermute | solution.py:463
  103.0 6.0 %collective-permute-done.14.arrived_ref = bf16[128,1536]{1,0:T(8,128)(2,1)S(1)} collective-permute-done((bf16[128,1536]{1,0:T(8,128)(2,1)S(1)}, bf16[128,1536]{1,0:T(8,128)(2,1)S(1)}, u32[]{:S(2)}, u32[]{:S(2)}) %collective-permute-start.14) | collective-permute-done | bytes 393248 | tf_op jit(solution)/shard_map/ppermute | solution.py:460
  109.8 1.6 %collective-permute-start.15 = (bf16[128,1536]{1,0:T(8,128)(2,1)}, bf16[128,1536]{1,0:T(8,128)(2,1)S(1)}, u32[]{:S(2)}, u32[]{:S(2)}) collective-permute-start(bf16[128,1536]{1,0:T(8,128)(2,1)} %join.5), channel_id=1, source_target_pairs={{0,2},{2,3},{3,1},{1,0},{4,6},{6,7},{7,5},{5,4},{8,10},{10,11},{11... | collective-permute-start | bytes 1179656 | tf_op jit(solution)/shard_map/ppermute | solution.py:460
  111.4 21.4 %stagger.1 = s32[1]{0:T(128)} custom-call(), custom_call_target="tpu_custom_call" | custom-call | tf_op jit(solution)/shard_map/stagger/pallas_call | solution.py:394
  (41 shorter events, 19.1 us)
Async XLA Ops:
  0.6 54.0 %copy-start = (bf16[1,256,1536]{2,1,0:T(8,128)(2,1)S(1)}, bf16[1,256,1536]{2,1,0:T(8,128)(2,1)}, u32[]{:S(2)}) copy-start(bf16[1,256,1536]{2,1,0:T(8,128)(2,1)} %param.5) | copy-start | bytes 2359300
  2.2 4.0 %collective-permute-start = (bf16[192,1536]{1,0:T(8,128)(2,1)S(1)}, bf16[192,1536]{1,0:T(8,128)(2,1)S(1)}, u32[]{:S(2)}, u32[]{:S(2)}) collective-permute-start(bf16[192,1536]{1,0:T(8,128)(2,1)S(1)} %reshape.16.refs_0_), channel_id=1, source_target_pairs={{0,4},{4,0},{8,12},{12,8},{16,20},{20,16},{24,28},{28,24},{1,5},{5... | collective-permute-start | bytes 1769480 | tf_op jit(solution)/shard_map/ppermute | solution.py:413
  2.3 27.8 %collective-permute-start.2 = (bf16[192,1536]{1,0:T(8,128)(2,1)S(1)}, bf16[192,1536]{1,0:T(8,128)(2,1)}, u32[]{:S(2)}, u32[]{:S(2)}) collective-permute-start(bf16[192,1536]{1,0:T(8,128)(2,1)S(1)} %reshape.16.refs_0_), channel_id=1, source_target_pairs={{0,16},{4,20},{8,24},{12,28},{16,0},{20,4},{24,8},{28,12},{1,17},{... | collective-permute-start | bytes 1769480 | tf_op jit(solution)/shard_map/ppermute | solution.py:413
  5.0 26.5 %collective-permute-start.1 = (bf16[192,1536]{1,0:T(8,128)(2,1)S(1)}, bf16[192,1536]{1,0:T(8,128)(2,1)S(1)}, u32[]{:S(2)}, u32[]{:S(2)}) collective-permute-start(bf16[192,1536]{1,0:T(8,128)(2,1)S(1)} %reshape.16.refs_0_), channel_id=1, source_target_pairs={{0,8},{4,12},{8,0},{12,4},{16,24},{20,28},{24,16},{28,20},{1,9},{5... | collective-permute-start | bytes 1769480 | tf_op jit(solution)/shard_map/ppermute | solution.py:413
  6.3 26.3 %collective-permute-start.3 = (bf16[192,1536]{1,0:T(8,128)(2,1)S(1)}, bf16[192,1536]{1,0:T(8,128)(2,1)}, u32[]{:S(2)}, u32[]{:S(2)}) collective-permute-start(bf16[192,1536]{1,0:T(8,128)(2,1)S(1)} %collective-permute-done.refs_1_), channel_id=1, source_target_pairs={{0,8},{4,12},{8,0},{12,4},{16,24},{20,28},{24,16},{28,20},{1,9},{5... | collective-permute-start | bytes 1769480 | tf_op jit(solution)/shard_map/ppermute | solution.py:413
  7.8 10.0 %collective-permute-start.7 = (bf16[128,1536]{1,0:T(8,128)(2,1)S(1)}, bf16[128,1536]{1,0:T(8,128)(2,1)S(1)}, u32[]{:S(2)}, u32[]{:S(2)}) collective-permute-start(bf16[128,1536]{1,0:T(8,128)(2,1)S(1)} %get-tuple-element.25), channel_id=1, source_target_pairs={{0,2},{2,3},{3,1},{1,0},{4,6},{6,7},{7,5},{5,4},{8,10},{10,11},{11... | collective-permute-start | bytes 1179656 | tf_op jit(solution)/shard_map/ppermute | solution.py:449
  10.2 16.1 %collective-permute-start.8 = (bf16[128,1536]{1,0:T(8,128)(2,1)S(1)}, bf16[128,1536]{1,0:T(8,128)(2,1)S(1)}, u32[]{:S(2)}, u32[]{:S(2)}) collective-permute-start(bf16[128,1536]{1,0:T(8,128)(2,1)S(1)} %get-tuple-element.24), channel_id=1, source_target_pairs={{0,2},{2,3},{3,1},{1,0},{4,6},{6,7},{7,5},{5,4},{8,10},{10,11},{11... | collective-permute-start | bytes 1179656 | tf_op jit(solution)/shard_map/ppermute | solution.py:449
  17.9 16.9 %collective-permute-start.9 = (bf16[128,1536]{1,0:T(8,128)(2,1)S(1)}, bf16[128,1536]{1,0:T(8,128)(2,1)}, u32[]{:S(2)}, u32[]{:S(2)}) collective-permute-start(bf16[128,1536]{1,0:T(8,128)(2,1)S(1)} %collective-permute-done.7.refs_9_), channel_id=1, source_target_pairs={{0,2},{2,3},{3,1},{1,0},{4,6},{6,7},{7,5},{5,4},{8,10},{10,11},{11... | collective-permute-start | bytes 1179656 | tf_op jit(solution)/shard_map/ppermute | solution.py:449
  26.3 16.9 %collective-permute-start.10 = (bf16[128,1536]{1,0:T(8,128)(2,1)S(1)}, bf16[128,1536]{1,0:T(8,128)(2,1)}, u32[]{:S(2)}, u32[]{:S(2)}) collective-permute-start(bf16[128,1536]{1,0:T(8,128)(2,1)S(1)} %collective-permute-done.8.refs_10_), channel_id=1, source_target_pairs={{0,2},{2,3},{3,1},{1,0},{4,6},{6,7},{7,5},{5,4},{8,10},{10,11},{11... | collective-permute-start | bytes 1179656 | tf_op jit(solution)/shard_map/ppermute | solution.py:449
  29.4 0.7 copy-start.3
  30.1 20.0 %collective-permute-start.4 = (bf16[192,1536]{1,0:T(8,128)(2,1)S(1)}, bf16[192,1536]{1,0:T(8,128)(2,1)}, u32[]{:S(2)}, u32[]{:S(2)}) collective-permute-start(bf16[192,1536]{1,0:T(8,128)(2,1)S(1)} %collective-permute-done.refs_1_), channel_id=1, source_target_pairs={{0,16},{4,20},{8,24},{12,28},{16,0},{20,4},{24,8},{28,12},{1,17},{... | collective-permute-start | bytes 1769480 | tf_op jit(solution)/shard_map/ppermute | solution.py:413
  31.5 0.8 copy-start.1
  32.3 17.9 %collective-permute-start.5 = (bf16[192,1536]{1,0:T(8,128)(2,1)}, bf16[192,1536]{1,0:T(8,128)(2,1)}, u32[]{:S(2)}, u32[]{:S(2)}) collective-permute-start(bf16[192,1536]{1,0:T(8,128)(2,1)} %collective-permute-done.2.refs_3_), channel_id=1, source_target_pairs={{0,8},{4,12},{8,0},{12,4},{16,24},{20,28},{24,16},{28,20},{1,9},{5... | collective-permute-start | bytes 1769480 | tf_op jit(solution)/shard_map/ppermute | solution.py:413
  32.5 22.1 %collective-permute-start.6 = (bf16[192,1536]{1,0:T(8,128)(2,1)}, bf16[192,1536]{1,0:T(8,128)(2,1)}, u32[]{:S(2)}, u32[]{:S(2)}) collective-permute-start(bf16[192,1536]{1,0:T(8,128)(2,1)} %collective-permute-done.3.refs_4_), channel_id=1, source_target_pairs={{0,16},{4,20},{8,24},{12,28},{16,0},{20,4},{24,8},{28,12},{1,17},{... | collective-permute-start | bytes 1769480 | tf_op jit(solution)/shard_map/ppermute | solution.py:413
  34.7 27.9 %collective-permute-start.11 = (bf16[128,1536]{1,0:T(8,128)(2,1)}, bf16[128,1536]{1,0:T(8,128)(2,1)}, u32[]{:S(2)}, u32[]{:S(2)}) collective-permute-start(bf16[128,1536]{1,0:T(8,128)(2,1)} %collective-permute-done.9.refs_11_), channel_id=1, source_target_pairs={{0,2},{2,3},{3,1},{1,0},{4,6},{6,7},{7,5},{5,4},{8,10},{10,11},{11... | collective-permute-start | bytes 1179656 | tf_op jit(solution)/shard_map/ppermute | solution.py:449
  43.1 19.5 %collective-permute-start.12 = (bf16[128,1536]{1,0:T(8,128)(2,1)}, bf16[128,1536]{1,0:T(8,128)(2,1)}, u32[]{:S(2)}, u32[]{:S(2)}) collective-permute-start(bf16[128,1536]{1,0:T(8,128)(2,1)} %collective-permute-done.10.refs_12_), channel_id=1, source_target_pairs={{0,2},{2,3},{3,1},{1,0},{4,6},{6,7},{7,5},{5,4},{8,10},{10,11},{11... | collective-permute-start | bytes 1179656 | tf_op jit(solution)/shard_map/ppermute | solution.py:449
  54.6 1.1 copy-start.2
  55.7 1.0 copy-start.4
  77.0 6.7 %collective-permute-start.16 = (bf16[128,1536]{1,0:T(8,128)(2,1)S(1)}, bf16[128,1536]{1,0:T(8,128)(2,1)S(1)}, u32[]{:S(2)}, u32[]{:S(2)}) collective-permute-start(bf16[128,1536]{1,0:T(8,128)(2,1)S(1)} %get-tuple-element.23), channel_id=1, source_target_pairs={{0,2},{2,3},{3,1},{1,0},{4,6},{6,7},{7,5},{5,4},{8,10},{10,11},{11... | collective-permute-start | bytes 1179656 | tf_op jit(solution)/shard_map/ppermute | solution.py:463
  77.7 14.5 %collective-permute-start.13 = (bf16[128,1536]{1,0:T(8,128)(2,1)S(1)}, bf16[128,1536]{1,0:T(8,128)(2,1)S(1)}, u32[]{:S(2)}, u32[]{:S(2)}) collective-permute-start(bf16[128,1536]{1,0:T(8,128)(2,1)S(1)} %get-tuple-element.20), channel_id=1, source_target_pairs={{0,2},{2,3},{3,1},{1,0},{4,6},{6,7},{7,5},{5,4},{8,10},{10,11},{11... | collective-permute-start | bytes 1179656 | tf_op jit(solution)/shard_map/ppermute | solution.py:460
  83.8 16.8 %collective-permute-start.17 = (bf16[128,1536]{1,0:T(8,128)(2,1)S(1)}, bf16[128,1536]{1,0:T(8,128)(2,1)S(1)}, u32[]{:S(2)}, u32[]{:S(2)}) collective-permute-start(bf16[128,1536]{1,0:T(8,128)(2,1)S(1)} %join.6), channel_id=1, source_target_pairs={{0,2},{2,3},{3,1},{1,0},{4,6},{6,7},{7,5},{5,4},{8,10},{10,11},{11... | collective-permute-start | bytes 1179656 | tf_op jit(solution)/shard_map/ppermute | solution.py:463
  92.2 16.8 %collective-permute-start.14 = (bf16[128,1536]{1,0:T(8,128)(2,1)S(1)}, bf16[128,1536]{1,0:T(8,128)(2,1)S(1)}, u32[]{:S(2)}, u32[]{:S(2)}) collective-permute-start(bf16[128,1536]{1,0:T(8,128)(2,1)S(1)} %join.4), channel_id=1, source_target_pairs={{0,2},{2,3},{3,1},{1,0},{4,6},{6,7},{7,5},{5,4},{8,10},{10,11},{11... | collective-permute-start | bytes 1179656 | tf_op jit(solution)/shard_map/ppermute | solution.py:460
  101.4 32.6 %collective-permute-start.18 = (bf16[128,1536]{1,0:T(8,128)(2,1)}, bf16[128,1536]{1,0:T(8,128)(2,1)S(1)}, u32[]{:S(2)}, u32[]{:S(2)}) collective-permute-start(bf16[128,1536]{1,0:T(8,128)(2,1)} %join.7), channel_id=1, source_target_pairs={{0,2},{2,3},{3,1},{1,0},{4,6},{6,7},{7,5},{5,4},{8,10},{10,11},{11... | collective-permute-start | bytes 1179656 | tf_op jit(solution)/shard_map/ppermute | solution.py:463
  109.8 24.1 %collective-permute-start.15 = (bf16[128,1536]{1,0:T(8,128)(2,1)}, bf16[128,1536]{1,0:T(8,128)(2,1)S(1)}, u32[]{:S(2)}, u32[]{:S(2)}) collective-permute-start(bf16[128,1536]{1,0:T(8,128)(2,1)} %join.5), channel_id=1, source_target_pairs={{0,2},{2,3},{3,1},{1,0},{4,6},{6,7},{7,5},{5,4},{8,10},{10,11},{11... | collective-permute-start | bytes 1179656 | tf_op jit(solution)/shard_map/ppermute | solution.py:460
